TPU v7x, 512 devices: a whole 4x4x16 slice. The times are simulated.
512 devices in a mesh: grp: 4 (over z_hi, core), row: 4 (over x), col: 32 (over y, z_lo).
Axes of the slice: x: 4, y: 4, z: 16 (z_hi: 2, z_lo: 8; z = z_hi * 8 + z_lo), core: 2. Of those that a mesh axis runs over, the one named last changes fastest.
Arguments:
- acts: bfloat16 [768, 8192], P('grp', 'col'), may hold values from -6 to 6
- grads: bfloat16 [768, 28672], P('grp', ('row', 'col')), may hold values from -6 to 6
- basis_in: bfloat16 [8192, 4096], P('col', 'row'), may hold values from -0.0625 to 0.0625
- basis_out: bfloat16 [4, 7168, 14336], P('row', 'grp', 'col'), may hold values from -0.03125 to 0.03125
- lengths: int32 [4, 2], P('grp'), may hold values from 1 to 96, 144 in all within a row
Outputs:
- eigenvalues: float32 [14336, 4096], P('col', 'row')
Inputs may be any that keep to these rules, and one draw needn't show every extreme that they name: The 2 lengths of each index of grp sum to exactly 144, and none exceeds 96.
All inputs are finite; a program needn't handle non-finite values.
Results may differ from a plain program's by a relative error of at most 0.006.
Values may be sent and summed in bfloat16 or wider, within the bound.
No kernel may reach another device: no remote copies, remote signals or barrier semaphores. Data moves between devices by JAX's collectives and lax.ppermute only.
A program may use at most 64 MiB of HBM per device.

v0:
```python
import jax
import jax.numpy as jnp
from jax import lax
from jax.sharding import PartitionSpec as P

LEN = 96
VALID = 144


def rows_for(lines, size):
    spare = -len(lines) % size
    return jnp.pad(lines, [(0, spare)] + [(0, 0)] * (lines.ndim - 1))


def sum_by_parts(value, axis):
    lines = value.reshape(-1, *value.shape[1:][-1:])
    own = lax.psum_scatter(
        rows_for(lines, lax.axis_size(axis)), axis, scatter_dimension=0, tiled=True
    )
    whole = lax.all_gather(own, axis).reshape(-1, *lines.shape[1:])
    return lax.slice_in_dim(whole, 0, len(lines)).reshape(value.shape)


def outer_square(left, right):
    block = lax.dot_general(
        left, right, (((0,), (0,)), ((), ())), preferred_element_type=jnp.float32
    )
    return block * block


def per_device(acts, grads, basis_in, basis_out, lengths):
    seq_lens = lengths[0]
    count = seq_lens.shape[0]
    partial_in = jnp.dot(acts, basis_in, preferred_element_type=jnp.float32)
    proj_in = lax.psum(partial_in, "col").astype(jnp.bfloat16)
    ends = jnp.cumsum(seq_lens)
    starts = ends - seq_lens
    slot_ids = jnp.arange(VALID, dtype=jnp.int32)
    segment = jnp.sum((slot_ids[:, None] >= ends[None, :]).astype(jnp.int32), axis=1)
    member = segment[:, None] == jnp.arange(count, dtype=jnp.int32)[None, :]
    offset = jnp.sum(jnp.where(member, starts[None, :], 0), axis=1)
    source = segment * LEN + slot_ids - offset
    packed = jnp.take(grads, source, axis=0)
    gathered = lax.all_gather(packed, "col", axis=1, tiled=True)
    proj_in = jnp.take(proj_in, source, axis=0)
    partial_out = jnp.dot(
        gathered,
        lax.all_gather(basis_out, "grp", axis=1, tiled=True)[0],
        preferred_element_type=jnp.float32,
    )
    proj_out = lax.psum(partial_out, "row").astype(jnp.bfloat16)
    slot_pos = jnp.arange(LEN, dtype=jnp.int32)
    total = jnp.zeros((proj_out.shape[1], proj_in.shape[1]), jnp.float32)
    padded_out = jnp.concatenate(
        [proj_out, jnp.zeros((LEN, proj_out.shape[1]), jnp.bfloat16)], axis=0
    )
    padded_in = jnp.concatenate([proj_in, jnp.zeros((LEN, proj_in.shape[1]), jnp.bfloat16)], axis=0)
    for seq in range(count):
        keep = (slot_pos < seq_lens[seq]).astype(jnp.bfloat16)
        piece_out = lax.dynamic_slice_in_dim(padded_out, starts[seq], LEN, 0)
        piece_in = lax.dynamic_slice_in_dim(padded_in, starts[seq], LEN, 0)
        total = total + outer_square(piece_out * keep[:, None], piece_in)
    summed = sum_by_parts(total.astype(jnp.bfloat16), "grp").astype(jnp.float32)
    return summed / (lax.axis_size("grp") * count * LEN)


def solution(mesh):
    in_specs = (
        P("grp", "col"),
        P("grp", ("row", "col")),
        P("col", "row"),
        P("row", "grp", "col"),
        P("grp", None),
    )
    out_specs = P("col", "row")
    return jax.shard_map(
        per_device, mesh=mesh, in_specs=in_specs, out_specs=out_specs, check_vma=False
    )
```

profile of v0, /device:TPU:3, one launch (start us, length us, event | category | flops | bytes accessed | tf_op | source)
XLA Modules:
  0.0 542.7 jit_solution(12668688378372334434)
XLA Ops:
  6.5 0.9 reduce-window.4
  7.4 0.7 fusion.13
  8.2 0.1 fusion.10
  8.3 1.7 gather_fusion
  10.0 0.7 select_bitcast_fusion
  10.8 0.7 all-gather.5.cloned.1.call-update
  11.6 0.6 fusion.17
  14.6 0.3 fusion.18
  14.9 229.0 %all-reduce.5 = bf16[192,1024]{1,0:T(8,128)(2,1)S(1)} all-reduce(f32[192,1024]{1,0:T(8,128)S(1)} %fusion.18), channel_id=1, replica_groups=mesh['grp'=4,'row'=4,'col'=32] {'col'}, use_global_device_ids=true, to_apply=%region_4.5 | all-reduce | flops 196608 | bytes 1179648 | tf_op jit(solution)/shard_map/psum | solution.py:35
  243.9 0.9 gather_fusion.1
  246.0 0.6 fusion.16
  246.6 0.6 compare_convert_fusion.2
  247.1 0.6 compare_convert_fusion.1
  247.8 0.1 broadcast_select_fusion
  247.9 2.5 copy.8
  250.4 5.0 reshape.92
  255.4 150.0 %all-gather.5.cloned.1.call-done = bf16[1,7168,448]{1,2,0:T(8,128)(2,1)} async-done(((bf16[1,1792,448]{1,2,0:T(8,128)(2,1)}), bf16[1,7168,448]{1,2,0:T(8,128)(2,1)}) %all-gather.5.cloned.1.call-update) | async-done | bytes 6422544 | tf_op jit(solution)/shard_map/all_gather | solution.py:48
  405.4 5.5 %fusion = f32[144,448]{1,0:T(8,128)S(1)} fusion(bf16[7168,144]{0,1:T(8,128)(2,1)} %reshape.92, bf16[1,7168,448]{1,2,0:T(8,128)(2,1)} %all-gather.5.cloned.1.call-done), kind=kOutput, calls=%fused_computation.2 | convolution fusion | flops 924844032 | bytes 8744960 | tf_op jit(solution)/shard_map/dot_general | solution.py:46
  410.9 25.5 %all-reduce.4 = bf16[144,448]{1,0:T(8,128)(2,1)S(1)} all-reduce(f32[144,448]{1,0:T(8,128)S(1)} %fusion), channel_id=1, replica_groups=mesh['grp'=4,'row'=4,'col'=32] {'row'}, use_global_device_ids=true, to_apply=%region_3.4 | all-reduce | flops 64512 | bytes 387072 | tf_op jit(solution)/shard_map/psum | solution.py:51
  436.4 0.5 fusion.2
  436.9 1.4 add_convert_fusion
  438.3 65.1 %reduce-scatter.2.cloned.1.call-done = bf16[112,1024]{1,0:T(8,128)(2,1)} async-done(((bf16[448,1024]{1,0:T(8,128)(2,1)}), bf16[112,1024]{1,0:T(8,128)(2,1)}) %reduce-scatter.2.cloned.1.call-update) | async-done | bytes 229392 | tf_op jit(solution)/shard_map/reduce_scatter | solution.py:17
  503.4 31.3 %all-gather = bf16[448,1024]{1,0:T(8,128)(2,1)S(1)} all-gather(bf16[112,1024]{1,0:T(8,128)(2,1)} %reduce-scatter.2.cloned.1.call-done), channel_id=2, replica_groups=mesh['grp'=4,'row'=4,'col'=32] {'grp'}, dimensions={0}, use_global_device_ids=true | all-gather | bytes 1146880 | tf_op jit(solution)/shard_map/all_gather | solution.py:20
  534.7 1.5 convert_multiply_fusion
  (18 shorter events, 0.3 us)
Async XLA Ops:
  6.5 8.0 %copy-start = (bf16[256,1024]{1,0:T(8,128)(2,1)S(1)}, bf16[256,1024]{1,0:T(8,128)(2,1)}, u32[]{:S(2)}) copy-start(bf16[256,1024]{1,0:T(8,128)(2,1)} %param.7) | copy-start | bytes 1572868
  6.5 5.0 copy-start.2
  6.5 8.1 %copy-start.1 = (bf16[192,256]{1,0:T(8,128)(2,1)S(1)}, bf16[192,256]{1,0:T(8,128)(2,1)}, u32[]{:S(2)}) copy-start(bf16[192,256]{1,0:T(8,128)(2,1)} %param.5) | copy-start | bytes 294916
  6.5 241.4 %all-gather.7.cloned.1.call-start = ((), (), s32[]{:S(2)}) async-start(), calls=%async_computation.3 | async-start | bytes 2433024 | tf_op jit(solution)/shard_map/all_gather | solution.py:44
  10.8 394.6 %all-gather.5.cloned.1.call-start = ((), (), s32[]{:S(2)}) async-start(), calls=%async_computation.1 | async-start | bytes 8028160 | tf_op jit(solution)/shard_map/all_gather | solution.py:48
  11.5 491.9 %reduce-scatter.2.cloned.1.call-start = ((), (), s32[]{:S(2)}) async-start(), calls=%async_computation.2 | async-start | bytes 1146880 | tf_op jit(solution)/shard_map/reduce_scatter | solution.py:17
Sparse Core Ops, SparseCore 0:
  10.9 215.8 all-gather.6
  228.9 176.4 all-gather.4
  438.5 64.9 reduce-scatter.1
where the time goes:
time: 543 us
  blocking collectives  286 us (53%)
  waiting for transfers between devices  216 us (40%)
  between operations  16.8 us (3%)
  local copies, waits for them, and re-layouts  11.3 us (2%)
  matrix products  7.65 us (1%)
    psum x1, blocking collectives, per_device(): proj_in = lax.psum(partial_in, 'col').astype(jnp.bfloat16)  229 us
    all_gather x1, waiting for transfers between devices, per_device(): lax.all_gather(basis_out, 'grp', axis=1, tiled=True)[0]  150 us
    reduce_scatter x1, waiting for transfers between devices, sum_by_parts(): lax.psum_scatter(rows_for(lines, lax.axis_size(axis)), axis, scatter_dime...  65.1 us
    all_gather x1, blocking collectives, sum_by_parts(): whole = lax.all_gather(own, axis).reshape(-1, *lines.shape[1:])  31.3 us
    psum x1, blocking collectives, per_device(): proj_out = lax.psum(partial_out, 'row').astype(jnp.bfloat16)  25.5 us
  transfers between devices with their start and end apart: 3, of which 2 were waited for; matrix products, arithmetic and copies ran while one was open for 2% of the time, Pallas kernels for 0%

commit v1 on v0

--- a/solution.py
+++ b/solution.py
@@ -5,6 +5,11 @@
 
 LEN = 96
 VALID = 144
+
+
+def gather_over(x, name, along):
+    sent = jnp.stack([x] * lax.axis_size(name))
+    return jnp.concatenate(lax.all_to_all(sent, name, 0, 0), axis=along)
 
 
 def rows_for(lines, size):
@@ -44,9 +49,7 @@
     gathered = lax.all_gather(packed, "col", axis=1, tiled=True)
     proj_in = jnp.take(proj_in, source, axis=0)
     partial_out = jnp.dot(
-        gathered,
-        lax.all_gather(basis_out, "grp", axis=1, tiled=True)[0],
-        preferred_element_type=jnp.float32,
+        gathered, gather_over(basis_out, "grp", 1)[0], preferred_element_type=jnp.float32
     )
     proj_out = lax.psum(partial_out, "row").astype(jnp.bfloat16)
     slot_pos = jnp.arange(LEN, dtype=jnp.int32)

time: 543 us -> 735 us (1.35)
  blocking collectives: 286 us -> 569 us
  waiting for transfers between devices: 216 us -> 94.3 us
  local copies, waits for them, and re-layouts: 11.3 us -> 29.9 us
  starting transfers between devices: 0.08 us -> 15.9 us
    psum x1, blocking collectives: 229 us -> 520 us  [per_device(): proj_in = lax.psum(partial_in, 'col').astype(jnp.bfloat16)]
    all_gather x1 -> x0, waiting for transfers between devices: 150 us -> none  [per_device(): lax.all_gather(basis_out, 'grp', axis=1, tiled=True)[0]]
    reduce_scatter x1, waiting for transfers between devices: 65.1 us -> 94.2 us  [sum_by_parts(): lax.psum_scatter(rows_for(lines, lax.axis_size(axis)), axis, scatter_dime...]
    all_to_all x0 -> x1, starting transfers between devices: none -> 15.9 us  [gather_over(): return jnp.concatenate(lax.all_to_all(sent, name, 0, 0), axis=along)]
    all_to_all x0 -> x1, local copies, waits for them, and re-layouts: none -> 10.5 us  [gather_over(): return jnp.concatenate(lax.all_to_all(sent, name, 0, 0), axis=along)]
    psum x1, blocking collectives: 25.5 us -> 17 us  [per_device(): proj_out = lax.psum(partial_out, 'row').astype(jnp.bfloat16)]
  transfers between devices with their start and end apart: 3 -> 3, of which waited for: 2 -> 1; matrix products, arithmetic and copies ran while one was open for 2% -> 2% of each run, Pallas kernels for 0% -> 0%
where the time goes in v1:
time: 735 us; the launch traced here: 734 us
  blocking collectives  569 us (77%)
  waiting for transfers between devices  94.3 us (13%)
  local copies, waits for them, and re-layouts  29.9 us (4%)
  between operations  17.5 us (2%)
  starting transfers between devices  15.9 us (2%)
    psum x1, blocking collectives, per_device(): proj_in = lax.psum(partial_in, 'col').astype(jnp.bfloat16)  520 us
    reduce_scatter x1, waiting for transfers between devices, sum_by_parts(): lax.psum_scatter(rows_for(lines, lax.axis_size(axis)), axis, scatter_dime...  94.2 us
    all_gather x1, blocking collectives, sum_by_parts(): whole = lax.all_gather(own, axis).reshape(-1, *lines.shape[1:])  31.3 us
    psum x1, blocking collectives, per_device(): proj_out = lax.psum(partial_out, 'row').astype(jnp.bfloat16)  17 us
    all_to_all x1, starting transfers between devices, gather_over(): return jnp.concatenate(lax.all_to_all(sent, name, 0, 0), axis=along)  15.9 us
  transfers between devices with their start and end apart: 3, of which 1 were waited for; matrix products, arithmetic and copies ran while one was open for 2% of the time, Pallas kernels for 0%

profile of v1, /device:TPU:3, one launch (start us, length us, event | category | flops | bytes accessed | tf_op | source)
XLA Modules:
  0.0 734.4 jit_solution(15074596825972032130)
XLA Ops:
  6.5 4.6 stack.2
  11.1 15.9 %all-to-all-start = ((bf16[4,1,1792,448]{2,3,1,0:T(8,128)(2,1)}), bf16[4,1,1792,448]{2,3,1,0:T(8,128)(2,1)}, u32[]{:S(2)}, u32[]{:S(2)}) async-start(bf16[4,1,1792,448]{2,3,1,0:T(8,128)(2,1)} %stack.2), calls=%async_computation | async-start | bytes 12845056 | tf_op jit(solution)/shard_map/all_to_all | solution.py:12
  27.0 0.2 reduce-window.4
  27.4 0.9 gather_fusion
  28.3 0.7 select_bitcast_fusion
  29.1 0.6 fusion.15
  32.4 0.3 fusion.17
  32.7 520.3 %all-reduce.5 = bf16[192,1024]{1,0:T(8,128)(2,1)S(1)} all-reduce(f32[192,1024]{1,0:T(8,128)S(1)} %fusion.17), channel_id=1, replica_groups=mesh['grp'=4,'row'=4,'col'=32] {'col'}, use_global_device_ids=true, to_apply=%region_4.5 | all-reduce | flops 196608 | bytes 1179648 | tf_op jit(solution)/shard_map/psum | solution.py:40
  553.0 0.9 gather_fusion.1
  555.2 0.6 fusion.14
  555.9 0.7 compare_convert_fusion.2
  556.6 0.6 compare_convert_fusion.1
  557.2 0.1 broadcast_select_fusion
  557.4 2.5 copy.12
  559.8 4.9 reshape.95
  564.8 10.5 %copy.13 = bf16[4,1,1792,448]{2,0,3,1:T(4,128)(2,1)} copy(bf16[4,1,1792,448]{2,3,1,0:T(8,128)(2,1)} %all-to-all-done) | data formatting | bytes 12845056 | tf_op jit(solution)/shard_map/all_to_all | solution.py:12
  575.2 4.3 copy.14
  579.6 2.0 fusion.16
  581.6 17.0 %all-reduce.4 = bf16[144,448]{1,0:T(8,128)(2,1)S(1)} all-reduce(f32[144,448]{1,0:T(8,128)S(1)} %fusion.16), channel_id=1, replica_groups=mesh['grp'=4,'row'=4,'col'=32] {'row'}, use_global_device_ids=true, to_apply=%region_3.4 | all-reduce | flops 64512 | bytes 387072 | tf_op jit(solution)/shard_map/psum | solution.py:54
  598.6 0.5 fusion
  599.1 1.4 add_convert_fusion
  600.5 94.2 %reduce-scatter.2.cloned.1.call-done = bf16[112,1024]{1,0:T(8,128)(2,1)} async-done(((bf16[448,1024]{1,0:T(8,128)(2,1)}), bf16[112,1024]{1,0:T(8,128)(2,1)}) %reduce-scatter.2.cloned.1.call-update) | async-done | bytes 229392 | tf_op jit(solution)/shard_map/reduce_scatter | solution.py:22
  694.8 31.3 %all-gather = bf16[448,1024]{1,0:T(8,128)(2,1)S(1)} all-gather(bf16[112,1024]{1,0:T(8,128)(2,1)} %reduce-scatter.2.cloned.1.call-done), channel_id=2, replica_groups=mesh['grp'=4,'row'=4,'col'=32] {'grp'}, dimensions={0}, use_global_device_ids=true | all-gather | bytes 1146880 | tf_op jit(solution)/shard_map/all_gather | solution.py:25
  726.1 1.5 convert_multiply_fusion
  (24 shorter events, 0.3 us)
Async XLA Ops:
  6.5 25.9 %copy-start = (bf16[256,1024]{1,0:T(8,128)(2,1)S(1)}, bf16[256,1024]{1,0:T(8,128)(2,1)}, u32[]{:S(2)}) copy-start(bf16[256,1024]{1,0:T(8,128)(2,1)} %param.7) | copy-start | bytes 1572868
  11.1 15.9 %copy-start.4 = (s32[1,2]{1,0:T(1,128)S(1)}, s32[1,2]{1,0:T(1,128)}, u32[]{:S(2)}) copy-start(s32[1,2]{1,0:T(1,128)} %param.9) | copy-start | bytes 28
  11.1 16.3 %copy-start.2 = (bf16[192,224]{1,0:T(8,128)(2,1)S(1)}, bf16[192,224]{1,0:T(8,128)(2,1)}, u32[]{:S(2)}) copy-start(bf16[192,224]{1,0:T(8,128)(2,1)} %param.6) | copy-start | bytes 258052
  11.1 21.3 %copy-start.3 = (bf16[192,256]{1,0:T(8,128)(2,1)S(1)}, bf16[192,256]{1,0:T(8,128)(2,1)}, u32[]{:S(2)}) copy-start(bf16[192,256]{1,0:T(8,128)(2,1)} %param.5) | copy-start | bytes 294916
  11.1 553.6 %all-to-all-start = ((bf16[4,1,1792,448]{2,3,1,0:T(8,128)(2,1)}), bf16[4,1,1792,448]{2,3,1,0:T(8,128)(2,1)}, u32[]{:S(2)}, u32[]{:S(2)}) async-start(bf16[4,1,1792,448]{2,3,1,0:T(8,128)(2,1)} %stack.2), calls=%async_computation | async-start | bytes 12845056 | tf_op jit(solution)/shard_map/all_to_all | solution.py:12
  27.0 530.3 %all-gather.4.cloned.1.call-start = ((), (), s32[]{:S(2)}) async-start(), calls=%async_computation.3 | async-start | bytes 2433024 | tf_op jit(solution)/shard_map/all_gather | solution.py:49
  29.1 665.7 %reduce-scatter.2.cloned.1.call-start = ((), (), s32[]{:S(2)}) async-start(), calls=%async_computation.2 | async-start | bytes 1146880 | tf_op jit(solution)/shard_map/reduce_scatter | solution.py:22
  575.2 4.3 copy-start.1
Sparse Core Ops, SparseCore 0:
  29.9 362.1 all-gather.3
  600.7 94.0 reduce-scatter.1

commit v2 on v0

--- a/solution.py
+++ b/solution.py
@@ -5,6 +5,11 @@
 
 LEN = 96
 VALID = 144
+
+
+def gather_and_add(x, mesh_axis):
+    parts = lax.all_gather(x, mesh_axis)
+    return jnp.sum(parts, axis=0)
 
 
 def rows_for(lines, size):
@@ -32,7 +37,7 @@
     seq_lens = lengths[0]
     count = seq_lens.shape[0]
     partial_in = jnp.dot(acts, basis_in, preferred_element_type=jnp.float32)
-    proj_in = lax.psum(partial_in, "col").astype(jnp.bfloat16)
+    proj_in = gather_and_add(partial_in, "col").astype(jnp.bfloat16)
     ends = jnp.cumsum(seq_lens)
     starts = ends - seq_lens
     slot_ids = jnp.arange(VALID, dtype=jnp.int32)

time: 543 us -> 1080 us (1.99)
  waiting for transfers between devices: 216 us -> 976 us
  blocking collectives: 286 us -> 50.6 us
    all_gather x0 -> x1, waiting for transfers between devices: none -> 535 us  [gather_and_add(): parts = lax.all_gather(x, mesh_axis)]
    psum x1 -> x0, blocking collectives: 229 us -> none  [per_device(): proj_in = lax.psum(partial_in, 'col').astype(jnp.bfloat16)]
    all_gather x1, waiting for transfers between devices: 0.02 us -> 205 us  [per_device(): gathered = lax.all_gather(packed, 'col', axis=1, tiled=True)]
    all_gather x1, waiting for transfers between devices: 150 us -> 173 us  [per_device(): lax.all_gather(basis_out, 'grp', axis=1, tiled=True)[0]]
  transfers between devices with their start and end apart: 3 -> 4, of which waited for: 2 -> 4; matrix products, arithmetic and copies ran while one was open for 2% -> 2% of each run, Pallas kernels for 0% -> 0%
where the time goes in v2:
time: 1080 us
  waiting for transfers between devices  976 us (90%)
  blocking collectives  50.6 us (5%)
  between operations  17.2 us (2%)
  other arithmetic  14.5 us (1%)
  local copies, waits for them, and re-layouts  11.3 us (1%)
    all_gather x1, waiting for transfers between devices, gather_and_add(): parts = lax.all_gather(x, mesh_axis)  535 us
    all_gather x1, waiting for transfers between devices, per_device(): gathered = lax.all_gather(packed, 'col', axis=1, tiled=True)  205 us
    all_gather x1, waiting for transfers between devices, per_device(): lax.all_gather(basis_out, 'grp', axis=1, tiled=True)[0]  173 us
    reduce_scatter x1, waiting for transfers between devices, sum_by_parts(): lax.psum_scatter(rows_for(lines, lax.axis_size(axis)), axis, scatter_dime...  62.9 us
    all_gather x1, blocking collectives, sum_by_parts(): whole = lax.all_gather(own, axis).reshape(-1, *lines.shape[1:])  31.3 us
  transfers between devices with their start and end apart: 4, of which 4 were waited for; matrix products, arithmetic and copies ran while one was open for 2% of the time, Pallas kernels for 0%

profile of v2, /device:TPU:3, one launch (start us, length us, event | category | flops | bytes accessed | tf_op | source)
XLA Modules:
  0.0 1078.5 jit_solution(3196047604749573972)
XLA Ops:
  6.5 0.9 reduce-window.4
  7.4 0.7 fusion.13
  8.3 1.7 gather_fusion
  10.0 0.7 select_bitcast_fusion
  10.8 0.7 all-gather.7.cloned.1.call-update
  11.6 1.2 fusion.18
  12.8 0.7 fusion.17
  17.4 0.7 fusion.16
  18.1 0.6 compare_convert_fusion.2
  18.7 0.7 compare_convert_fusion.1
  19.4 204.9 %all-gather.11.cloned.1.call-done = bf16[32,224,144]{1,2,0:T(8,128)(2,1)} async-done(((bf16[1,224,144]{1,2,0:T(8,128)(2,1)}), bf16[32,224,144]{1,2,0:T(8,128)(2,1)}) %all-gather.11.cloned.1.call-update) | async-done | bytes 2064400 | tf_op jit(solution)/shard_map/all_gather | solution.py:49
  224.3 2.5 copy.8
  226.8 4.9 reshape.93
  231.7 172.8 %all-gather.7.cloned.1.call-done = bf16[1,7168,448]{1,2,0:T(8,128)(2,1)} async-done(((bf16[1,1792,448]{1,2,0:T(8,128)(2,1)}), bf16[1,7168,448]{1,2,0:T(8,128)(2,1)}) %all-gather.7.cloned.1.call-update) | async-done | bytes 6422544 | tf_op jit(solution)/shard_map/all_gather | solution.py:53
  404.5 5.5 fusion
  410.0 19.4 %all-reduce.3 = bf16[144,448]{1,0:T(8,128)(2,1)S(1)} all-reduce(f32[144,448]{1,0:T(8,128)S(1)} %fusion), channel_id=1, replica_groups=mesh['grp'=4,'row'=4,'col'=32] {'row'}, use_global_device_ids=true, to_apply=%region_3.4 | all-reduce | flops 64512 | bytes 387072 | tf_op jit(solution)/shard_map/psum | solution.py:56
  429.4 534.8 %all-gather.9.cloned.1.call-done = f32[6144,1024]{1,0:T(8,128)} async-done(((f32[192,1024]{1,0:T(8,128)}), f32[6144,1024]{1,0:T(8,128)}) %all-gather.9.cloned.1.call-update) | async-done | bytes 25165840 | tf_op jit(solution)/shard_map/all_gather | solution.py:11
  964.2 9.2 reduce_sum.32
  973.3 0.9 gather_fusion.1
  974.4 0.5 fusion.2
  974.9 1.4 add_convert_fusion
  976.3 62.9 %reduce-scatter.2.cloned.1.call-done = bf16[112,1024]{1,0:T(8,128)(2,1)} async-done(((bf16[448,1024]{1,0:T(8,128)(2,1)}), bf16[112,1024]{1,0:T(8,128)(2,1)}) %reduce-scatter.2.cloned.1.call-update) | async-done | bytes 229392 | tf_op jit(solution)/shard_map/reduce_scatter | solution.py:22
  1039.2 31.3 %all-gather.1 = bf16[448,1024]{1,0:T(8,128)(2,1)S(1)} all-gather(bf16[112,1024]{1,0:T(8,128)(2,1)} %reduce-scatter.2.cloned.1.call-done), channel_id=3, replica_groups=mesh['grp'=4,'row'=4,'col'=32] {'grp'}, dimensions={0}, use_global_device_ids=true | all-gather | bytes 1146880 | tf_op jit(solution)/shard_map/all_gather | solution.py:25
  1070.5 1.5 convert_multiply_fusion
  (21 shorter events, 0.5 us)
Async XLA Ops:
  6.5 5.0 copy-start
  6.5 5.0 copy-start.1
  6.5 217.8 %all-gather.11.cloned.1.call-start = ((), (), s32[]{:S(2)}) async-start(), calls=%async_computation.4 | async-start | bytes 2433024 | tf_op jit(solution)/shard_map/all_gather | solution.py:49
  10.8 2.1 copy-start.2
  10.8 393.8 %all-gather.7.cloned.1.call-start = ((), (), s32[]{:S(2)}) async-start(), calls=%async_computation.1 | async-start | bytes 8028160 | tf_op jit(solution)/shard_map/all_gather | solution.py:53
  11.5 952.6 %all-gather.9.cloned.1.call-start = ((), (), s32[]{:S(2)}) async-start(), calls=%async_computation.3 | async-start | bytes 25952256 | tf_op jit(solution)/shard_map/all_gather | solution.py:11
  12.8 1026.5 %reduce-scatter.2.cloned.1.call-start = ((), (), s32[]{:S(2)}) async-start(), calls=%async_computation.2 | async-start | bytes 1146880 | tf_op jit(solution)/shard_map/reduce_scatter | solution.py:22
Sparse Core Ops, SparseCore 0:
  10.9 213.4 all-gather.10
  226.4 178.0 all-gather.6
  406.6 557.5 all-gather.8
  976.4 62.7 reduce-scatter.1
